TPU v7x, 256 devices: a whole 4x4x8 slice. The times are simulated.
256 devices in a mesh: dp: 32 (over z, y), ctx: 8 (over x, core).
Axes of the slice: x: 4, y: 4, z: 8, core: 2. Of those that a mesh axis runs over, the one named last changes fastest.
Arguments:
- query_rows: bfloat16 [32768, 2048], P(('dp', 'ctx')), may hold values from -6 to 6
- key_rows: bfloat16 [32768, 2048], P(('dp', 'ctx')), may hold values from -6 to 6
- value_rows: bfloat16 [32768, 2048], P(('dp', 'ctx')), may hold values from -6 to 6
- target: bfloat16 [32768, 1536], P(('dp', 'ctx')), may hold values from -18 to 18
- w_out: bfloat16 [2048, 1536], replicated, may hold values from -0.125 to 0.125
- clip_lengths: int32 [32, 4], P('dp'), may hold values from 1 to 512, 1024 in all within a row
- timesteps: int32 [32, 4], P('dp'), may hold values from 0 to 999
- tile_pattern: int32 [32, 8, 8], P('dp'), may hold values 0 or 1
- tau_prev: float32 [1], replicated, may hold values from 1 to 4
Outputs:
- query_grad: bfloat16 [32768, 2048], P(('dp', 'ctx'))
- key_grad: bfloat16 [32768, 2048], P(('dp', 'ctx'))
- value_grad: bfloat16 [32768, 2048], P(('dp', 'ctx'))
- weight_grad: float32 [2048, 1536], P('ctx', 'dp')
Inputs may be any that keep to these rules, and one draw needn't show every extreme that they name: `clip_lengths`: each row of clip lengths sums to 1024, and its largest entry is 512.
All inputs are finite; a program needn't handle non-finite values. No bound on the sum of `tile_pattern` on one device may be relied on, other than what follows from the above.
Results may differ from a plain program's by a relative error of at most 0.019.
Values may be sent and summed in bfloat16 or wider, within the bound.
No kernel may reach another device: no remote copies, remote signals or barrier semaphores. Data moves between devices by JAX's collectives and lax.ppermute only.
A program may use at most 128 MiB of HBM per device.

v0:
```python
import math
import jax
import jax.numpy as jnp
from jax import lax
from jax.sharding import Mesh
from jax.sharding import PartitionSpec as P

HD = 128
OUT = 1536
CLIPS = 4
TILE = 128
DP = ("dp_0", "dp_1")
DP_CTX = ("dp_0", "dp_1", "ctx")
MOMENTUM = 0.9


def sent_to_all(array, axis):
    copies = jnp.broadcast_to(array, (lax.axis_size(axis), *array.shape))
    return lax.all_to_all(copies, axis, split_axis=0, concat_axis=0, tiled=True)


def over_copies(array, axis):
    everything = sent_to_all(array, axis)
    return jnp.sum(everything, axis=0)


def summed_rows(array, axes, dim):
    if not axes:
        return array
    nearer = lax.psum_scatter(array, axes[0], scatter_dimension=dim, tiled=True)
    return summed_rows(nearer, axes[1:], dim)


def clip_index(lengths_row, positions):
    ends = jnp.cumsum(lengths_row)
    return jnp.sum((positions[:, None] >= ends[None, :]).astype(jnp.int32), axis=1)


def attention_mask(clip_ids, pattern, row_total):
    tiles = row_total // TILE
    tile_ok = (
        jnp.broadcast_to(pattern[:, None, :, None], (tiles, TILE, tiles, TILE)).reshape(
            row_total, row_total
        )
        > 0
    )
    tile_ids = jnp.arange(row_total, dtype=jnp.int32) // TILE
    same_tile = tile_ids[:, None] == tile_ids[None, :]
    return (clip_ids[:, None] == clip_ids[None, :]) & (tile_ok | same_tile)


def head_probs(query_head, key_head, allowed):
    score_scale = 1.0 / math.sqrt(HD)
    scores = (
        lax.dot_general(
            query_head, key_head, (((1,), (1,)), ((), ())), preferred_element_type=jnp.float32
        )
        * score_scale
    )
    scores = jnp.where(allowed, scores, -1e30)
    row_max = jnp.max(scores, axis=1)
    unnorm = jnp.where(allowed, jnp.exp(scores - row_max[:, None]), 0.0)
    row_total = jnp.sum(unnorm, axis=1)
    return unnorm / row_total[:, None]


def head_backward(query_head, key_head, value_head, out_head, grad_head, allowed):
    score_scale = 1.0 / math.sqrt(HD)
    probs = head_probs(query_head, key_head, allowed)
    probs_low = probs.astype(jnp.bfloat16)
    value_grad = lax.dot_general(
        probs_low, grad_head, (((0,), (0,)), ((), ())), preferred_element_type=jnp.float32
    ).astype(jnp.bfloat16)
    prob_grad = lax.dot_general(
        grad_head, value_head, (((1,), (1,)), ((), ())), preferred_element_type=jnp.float32
    )
    delta = jnp.sum(grad_head.astype(jnp.float32) * out_head.astype(jnp.float32), axis=1)
    score_grad = (probs * (prob_grad - delta[:, None])).astype(jnp.bfloat16)
    query_grad = (
        jnp.dot(score_grad, key_head, preferred_element_type=jnp.float32) * score_scale
    ).astype(jnp.bfloat16)
    key_grad = (
        lax.dot_general(
            score_grad, query_head, (((0,), (0,)), ((), ())), preferred_element_type=jnp.float32
        )
        * score_scale
    ).astype(jnp.bfloat16)
    return (query_grad, key_grad, value_grad)


def superloss_weight(clip_loss, tau_now):
    argument = jnp.maximum(-0.3, 0.5 * (clip_loss - tau_now))
    branch = jnp.log1p(argument)
    for sweep in range(5):
        exp_value = jnp.exp(branch)
        branch = branch - (branch * exp_value - argument) / (exp_value * (branch + 1.0))
    return jnp.exp(-branch)


def on_device(
    query_rows, key_rows, value_rows, target, w_out, clip_lengths, timesteps, tile_pattern, tau_prev
):
    row_count = query_rows.shape[0]
    ctx_count = lax.axis_size("ctx")
    dp_count = lax.axis_size(DP)
    pack_rows = row_count * ctx_count
    ctx_place = lax.axis_index("ctx")
    query_head, key_head, value_head = (
        lax.all_to_all(query_rows, "ctx", split_axis=1, concat_axis=0, tiled=True),
        lax.all_to_all(key_rows, "ctx", split_axis=1, concat_axis=0, tiled=True),
        lax.all_to_all(value_rows, "ctx", split_axis=1, concat_axis=0, tiled=True),
    )
    lengths_row = clip_lengths[0]
    clip_pack = clip_index(lengths_row, jnp.arange(pack_rows, dtype=jnp.int32))
    allowed = attention_mask(clip_pack, tile_pattern[0], pack_rows)
    width_dev = query_head.shape[1]
    heads_dev = width_dev // HD
    head_outs = []
    for head in range(heads_dev):
        cols = slice(head * HD, (head + 1) * HD)
        probs = head_probs(query_head[:, cols], key_head[:, cols], allowed)
        head_outs.append(
            jnp.dot(
                probs.astype(jnp.bfloat16), value_head[:, cols], preferred_element_type=jnp.float32
            ).astype(jnp.bfloat16)
        )
    out_head = jnp.concatenate(head_outs, axis=1)
    out_rows = lax.all_to_all(out_head, "ctx", split_axis=0, concat_axis=1, tiled=True)
    predicted = jnp.dot(out_rows, w_out, preferred_element_type=jnp.float32)
    residue = predicted - target.astype(jnp.float32)
    row_squares = jnp.sum(residue * residue, axis=1)
    positions = ctx_place * row_count + jnp.arange(row_count, dtype=jnp.int32)
    clip_rows = clip_index(lengths_row, positions)
    onehot = (clip_rows[:, None] == jnp.arange(CLIPS, dtype=jnp.int32)[None, :]).astype(jnp.float32)
    partial_value = jnp.sum(row_squares[:, None] * onehot, axis=0)
    clip_len = lengths_row.astype(jnp.float32)
    step_weight = 1.0 + timesteps[0].astype(jnp.float32) / 250.0
    clip_sq = over_copies(partial_value, "ctx")
    clip_loss = step_weight * clip_sq / (clip_len * OUT)
    loss_sum = over_copies(jnp.sum(clip_loss), DP)
    loss_mean = loss_sum / (dp_count * CLIPS)
    tau_now = MOMENTUM * tau_prev[0] + (1.0 - MOMENTUM) * loss_mean
    confidence = superloss_weight(clip_loss, tau_now)
    tokens_all = pack_rows * dp_count
    clip_scale = confidence * step_weight
    row_scale = jnp.sum(onehot * clip_scale[None, :], axis=1)
    pred_grad = (residue * row_scale[:, None]).astype(jnp.bfloat16)
    norm_factor = 1.0 / math.sqrt(tokens_all)
    pred_pack = lax.all_gather(pred_grad, "ctx", axis=0, tiled=True)
    w_block = lax.dynamic_slice_in_dim(w_out, ctx_place * width_dev, width_dev, 0)
    grad_head = lax.dot_general(
        pred_pack, w_block, (((1,), (1,)), ((), ())), preferred_element_type=jnp.float32
    ).astype(jnp.bfloat16)
    block_terms = (
        lax.dot_general(
            out_head, pred_pack, (((0,), (0,)), ((), ())), preferred_element_type=jnp.float32
        )
        * norm_factor
    )
    weight_grad = summed_rows(block_terms.astype(jnp.bfloat16), DP, 1).astype(jnp.float32)
    parts_q, parts_k, parts_v = ([], [], [])
    for head in range(heads_dev):
        cols = slice(head * HD, (head + 1) * HD)
        grads = head_backward(
            query_head[:, cols],
            key_head[:, cols],
            value_head[:, cols],
            out_head[:, cols],
            grad_head[:, cols],
            allowed,
        )
        parts_q.append(grads[0])
        parts_k.append(grads[1])
        parts_v.append(grads[2])
    query_back, key_back, value_back = (
        lax.all_to_all(
            jnp.concatenate(parts_q, axis=1), "ctx", split_axis=0, concat_axis=1, tiled=True
        ),
        lax.all_to_all(
            jnp.concatenate(parts_k, axis=1), "ctx", split_axis=0, concat_axis=1, tiled=True
        ),
        lax.all_to_all(
            jnp.concatenate(parts_v, axis=1), "ctx", split_axis=0, concat_axis=1, tiled=True
        ),
    )
    return (query_back, key_back, value_back, weight_grad)


def solution(mesh):
    finer = Mesh(mesh.devices.reshape(8, 4, mesh.shape["ctx"]), ("dp_0", "dp_1", "ctx"))
    return jax.shard_map(
        on_device,
        mesh=finer,
        in_specs=(
            P(DP_CTX, None),
            P(DP_CTX, None),
            P(DP_CTX, None),
            P(DP_CTX, None),
            P(),
            P(DP, None),
            P(DP, None),
            P(DP, None, None),
            P(),
        ),
        out_specs=(P(DP_CTX, None), P(DP_CTX, None), P(DP_CTX, None), P("ctx", DP)),
        check_vma=False,
    )
```

profile of v0, /device:TPU:4, one launch (start us, length us, event | category | flops | bytes accessed | tf_op | source)
XLA Modules:
  0.0 216.0 jit_solution(11657505855100650030)
XLA Ops:
  7.2 2.1 copy.72
  9.3 5.6 %all-to-all-start = ((bf16[128,8,256]{0,2,1:T(8,128)(2,1)}), bf16[128,8,256]{0,2,1:T(8,128)(2,1)S(1)}, u32[]{:S(2)}, u32[]{:S(2)}) async-start(bf16[128,8,256]{0,2,1:T(8,128)(2,1)} %bitcast.3), calls=%async_computation | async-start | bytes 1048576 | tf_op jit(solution)/shard_map/all_to_all | solution.py:109
  14.9 2.0 copy.74
  17.0 5.1 %all-to-all-done = bf16[128,8,256]{0,2,1:T(8,128)(2,1)S(1)} async-done(((bf16[128,8,256]{0,2,1:T(8,128)(2,1)}), bf16[128,8,256]{0,2,1:T(8,128)(2,1)S(1)}, u32[]{:S(2)}, u32[]{:S(2)}) %all-to-all-start) | async-done | bytes 524320 | tf_op jit(solution)/shard_map/all_to_all | solution.py:109
  22.1 6.6 %all-to-all-start.1 = ((bf16[128,8,256]{0,2,1:T(8,128)(2,1)}), bf16[128,8,256]{0,2,1:T(8,128)(2,1)S(1)}, u32[]{:S(2)}, u32[]{:S(2)}) async-start(bf16[128,8,256]{0,2,1:T(8,128)(2,1)} %bitcast.6), calls=%async_computation.1 | async-start | bytes 1048576 | tf_op jit(solution)/shard_map/all_to_all | solution.py:110
  29.7 6.2 %all-to-all-done.1 = bf16[128,8,256]{0,2,1:T(8,128)(2,1)S(1)} async-done(((bf16[128,8,256]{0,2,1:T(8,128)(2,1)}), bf16[128,8,256]{0,2,1:T(8,128)(2,1)S(1)}, u32[]{:S(2)}, u32[]{:S(2)}) %all-to-all-start.1) | async-done | bytes 524320 | tf_op jit(solution)/shard_map/all_to_all | solution.py:110
  35.8 6.6 %all-to-all-start.2 = ((bf16[128,8,256]{0,2,1:T(8,128)(2,1)}), bf16[128,8,256]{0,2,1:T(8,128)(2,1)S(1)}, u32[]{:S(2)}, u32[]{:S(2)}) async-start(bf16[128,8,256]{0,2,1:T(8,128)(2,1)} %bitcast.9), calls=%async_computation.2 | async-start | bytes 1048576 | tf_op jit(solution)/shard_map/all_to_all | solution.py:111
  43.2 6.3 %all-to-all-done.2 = bf16[128,8,256]{0,2,1:T(8,128)(2,1)S(1)} async-done(((bf16[128,8,256]{0,2,1:T(8,128)(2,1)}), bf16[128,8,256]{0,2,1:T(8,128)(2,1)S(1)}, u32[]{:S(2)}, u32[]{:S(2)}) %all-to-all-start.2) | async-done | bytes 524320 | tf_op jit(solution)/shard_map/all_to_all | solution.py:111
  50.9 2.5 %fusion.1 = (f32[1024]{0:T(1024)S(1)}, f32[1024]{0:T(1024)S(1)}, pred[1024,1024]{0,1:T(32,128)(4,1)S(1)}, f32[1024,1024]{0,1:T(8,128)S(1)}) fusion(f32[1024,1024]{0,1:T(8,128)S(1)} %fusion.21, s32[1024]{0:T(1024)S(1)} %add_select_fusion, pred[128,8,8,128]{3,2,1,0:T(8,128)(4,1)S(1)} %bitcast.96, s32[1024]{0:T(1024)S(1)} %convert_reduce_fusion, ...), kind=kOutput, calls=%fused_computation.8 | convolution fusion | flops 278919168 | bytes 11034624 | tf_op jit(solution)/shard_map/dot_general | solution.py:55
  53.4 2.2 %fusion.5 = (f32[1024]{0:T(1024)S(1)}, f32[1024]{0:T(1024)S(1)}) fusion(pred[1024,1024]{0,1:T(32,128)(4,1)S(1)} %get-tuple-element.22, f32[1024,1024]{0,1:T(8,128)S(1)} %get-tuple-element.23, f32[1024]{0:T(1024)S(1)} %get-tuple-element.18, f32[1024]{0:T(1024)S(1)} %get-tuple-element.19, f32[1024,1024]{0,1:T(8,128)S(1)} %fusion.21), kind=kLoop, calls=%fused_computation.14 | loop fusion | flops 10483712 | bytes 9453568 | tf_op jit(solution)/shard_map/reduce_sum | solution.py:63
  55.6 1.5 convolution_convert_fusion.3
  57.2 1.5 convolution_convert_fusion.4
  59.6 6.6 %all-to-all-start.3 = ((bf16[8,128,256]{1,2,0:T(8,128)(2,1)}), bf16[8,128,256]{1,2,0:T(8,128)(2,1)S(1)}, u32[]{:S(2)}, u32[]{:S(2)}) async-start(bf16[8,128,256]{1,2,0:T(8,128)(2,1)} %copy_bitcast_fusion.3), calls=%async_computation.3 | async-start | bytes 1048576 | tf_op jit(solution)/shard_map/all_to_all | solution.py:128
  66.3 7.1 %all-to-all-done.3 = bf16[8,128,256]{1,2,0:T(8,128)(2,1)S(1)} async-done(((bf16[8,128,256]{1,2,0:T(8,128)(2,1)}), bf16[8,128,256]{1,2,0:T(8,128)(2,1)S(1)}, u32[]{:S(2)}, u32[]{:S(2)}) %all-to-all-start.3) | async-done | bytes 524320 | tf_op jit(solution)/shard_map/all_to_all | solution.py:128
  73.4 3.9 %multiply_reduce_fusion = (f32[128]{0:T(128)S(1)}, f32[128,1536]{1,0:T(8,128)S(1)}) fusion(bf16[128,1536]{1,0:T(8,128)(2,1)} %param.12, bf16[128,2048]{0,1:T(8,128)(2,1)S(1)} %bitcast.85, bf16[2048,1536]{1,0:T(8,128)(2,1)} %param.13), kind=kOutput, calls=%fused_computation.36 | convolution fusion | flops 806092672 | bytes 7995904 | tf_op jit(solution)/shard_map/dot_general | solution.py:129
  77.4 8.4 %all_to_all.145 = f32[8,1,4]{2,1,0:T(1,128)S(1)} all-to-all(f32[8,1,4]{2,1,0:T(1,128)S(1)} %broadcast_in_dim.22), channel_id=1, replica_groups=mesh['dp_0'=8,'dp_1'=4,'ctx'=8] {'ctx'}, dimensions={0} | all-to-all | bytes 256 | tf_op jit(solution)/shard_map/all_to_all | solution.py:19
  87.8 10.7 %all-to-all-start.5 = ((f32[32,1,1]{2,1,0:T(1,128)}), f32[32,1,1]{2,1,0:T(1,128)S(1)}, u32[]{:S(2)}, u32[]{:S(2)}) async-start(f32[32,1,1]{2,1,0:T(1,128)} %broadcast_in_dim.23), calls=%async_computation.5 | async-start | bytes 32768 | tf_op jit(solution)/shard_map/all_to_all | solution.py:19
  99.1 9.0 %all-to-all-done.5 = f32[32,1,1]{2,1,0:T(1,128)S(1)} async-done(((f32[32,1,1]{2,1,0:T(1,128)}), f32[32,1,1]{2,1,0:T(1,128)S(1)}, u32[]{:S(2)}, u32[]{:S(2)}) %all-to-all-start.5) | async-done | bytes 160 | tf_op jit(solution)/shard_map/all_to_all | solution.py:19
  110.7 23.2 %all-gather.2.cloned.1.call-done = bf16[1024,1536]{1,0:T(8,128)(2,1)} async-done(((bf16[128,1536]{1,0:T(8,128)(2,1)}), bf16[1024,1536]{1,0:T(8,128)(2,1)}) %all-gather.2.cloned.1.call-update) | async-done | bytes 3145744 | tf_op jit(solution)/shard_map/all_gather | solution.py:149
  133.9 3.2 %convolution_convert_fusion = bf16[1024,256]{0,1:T(8,128)(2,1)S(1)} fusion(bf16[1024,1536]{1,0:T(8,128)(2,1)} %all-gather.2.cloned.1.call-done, bf16[2048,1536]{1,0:T(8,128)(2,1)} %param.13, s32[]{:T(128)S(6)} %select_n.38), kind=kOutput, calls=%fused_computation.17 | convolution fusion | flops 805568512 | bytes 4456452 | tf_op jit(solution)/shard_map/dot_general | solution.py:151
  137.3 1.5 convolution_convert_fusion.2
  139.7 1.5 convolution_convert_fusion.1
  141.6 2.3 %fusion.3 = bf16[256,1536]{0,1:T(8,128)(2,1)} fusion(bf16[1024,1536]{1,0:T(8,128)(2,1)S(1)} %copy-done.19, bf16[1024,128]{0,1:T(8,128)(2,1)S(1)} %convolution_convert_fusion.3, bf16[1024,128]{0,1:T(8,128)(2,1)S(1)} %convolution_convert_fusion.4), kind=kOutput, calls=%fused_computation.11 | convolution fusion | flops 807141376 | bytes 4456448 | tf_op jit(solution)/shard_map/dot_general | solution.py:155
  144.8 5.3 %all-to-all-start.8 = ((bf16[8,128,256]{1,2,0:T(8,128)(2,1)}), bf16[8,128,256]{1,2,0:T(8,128)(2,1)S(1)}, u32[]{:S(2)}, u32[]{:S(2)}) async-start(bf16[8,128,256]{1,2,0:T(8,128)(2,1)} %copy_bitcast_fusion), calls=%async_computation.8 | async-start | bytes 1048576 | tf_op jit(solution)/shard_map/all_to_all | solution.py:182
  150.2 5.1 %multiply_convert_fusion.1 = bf16[1024,1024]{0,1:T(8,128)(2,1)S(1)} fusion(f32[1024]{0:T(1024)S(1)} %get-tuple-element.20, bf16[1024,256]{1,0:T(8,128)(2,1)} %bitcast.99, bf16[1024,256]{0,1:T(8,128)(2,1)} %copy-done.14, f32[1024]{0:T(1024)S(1)} %get-tuple-element.16, pred[1024,1024]{0,1:T(32,128)(4,1)} %copy-done.9, f32[1024]{0:T(1024)S(1)} %get-tuple-element.18, ...), kind=kOutput, calls=%fused_computation.1 | convolution fusion | flops 276824064 | bytes 7876608 | tf_op jit(solution)/shard_map/dot_general | solution.py:74
  155.3 1.7 multiply_convert_fusion
  159.7 4.8 %all-to-all-start.7 = ((bf16[8,128,256]{1,2,0:T(8,128)(2,1)}), bf16[8,128,256]{1,2,0:T(8,128)(2,1)S(1)}, u32[]{:S(2)}, u32[]{:S(2)}) async-start(bf16[8,128,256]{1,2,0:T(8,128)(2,1)} %copy_bitcast_fusion.1), calls=%async_computation.7 | async-start | bytes 1048576 | tf_op jit(solution)/shard_map/all_to_all | solution.py:179
  164.5 1.6 fusion.8
  167.6 4.0 %all-to-all-done.7 = bf16[8,128,256]{1,2,0:T(8,128)(2,1)S(1)} async-done(((bf16[8,128,256]{1,2,0:T(8,128)(2,1)}), bf16[8,128,256]{1,2,0:T(8,128)(2,1)S(1)}, u32[]{:S(2)}, u32[]{:S(2)}) %all-to-all-start.7) | async-done | bytes 524320 | tf_op jit(solution)/shard_map/all_to_all | solution.py:179
  171.6 6.6 %all-to-all-start.6 = ((bf16[8,128,256]{1,2,0:T(8,128)(2,1)}), bf16[8,128,256]{1,2,0:T(8,128)(2,1)S(1)}, u32[]{:S(2)}, u32[]{:S(2)}) async-start(bf16[8,128,256]{1,2,0:T(8,128)(2,1)} %copy_bitcast_fusion.2), calls=%async_computation.6 | async-start | bytes 1048576 | tf_op jit(solution)/shard_map/all_to_all | solution.py:176
  178.2 5.6 %reduce-scatter.3.cloned.1.call-done = bf16[256,192]{0,1:T(8,128)(2,1)} async-done(((bf16[256,1536]{0,1:T(8,128)(2,1)}), bf16[256,192]{0,1:T(8,128)(2,1)}) %reduce-scatter.3.cloned.1.call-update) | async-done | bytes 98320 | tf_op jit(solution)/shard_map/reduce_scatter | solution.py:30
  186.8 21.3 %reduce-scatter.5.cloned.1.call-done = bf16[256,48]{0,1:T(8,128)(2,1)} async-done(((bf16[256,192]{0,1:T(8,128)(2,1)}), bf16[256,48]{0,1:T(8,128)(2,1)}) %reduce-scatter.5.cloned.1.call-update) | async-done | bytes 24592 | tf_op jit(solution)/shard_map/reduce_scatter | solution.py:30
  (82 shorter events, 18.8 us)
Async XLA Ops:
  7.2 21.5 %copy-start.11 = (bf16[128,2048]{1,0:T(8,128)(2,1)S(1)}, bf16[128,2048]{1,0:T(8,128)(2,1)}, u32[]{:S(2)}) copy-start(bf16[128,2048]{1,0:T(8,128)(2,1)} %param.11) | copy-start | bytes 1572868
  7.2 35.2 %copy-start.16 = (s32[1,8,8]{2,1,0:T(8,128)S(1)}, s32[1,8,8]{2,1,0:T(8,128)}, u32[]{:S(2)}) copy-start(s32[1,8,8]{2,1,0:T(8,128)} %param.16) | copy-start | bytes 772
  7.2 35.3 %copy-start.17 = (s32[1,4]{1,0:T(1,128)S(1)}, s32[1,4]{1,0:T(1,128)}, u32[]{:S(2)}) copy-start(s32[1,4]{1,0:T(1,128)} %param.14) | copy-start | bytes 52
  9.3 12.8 %all-to-all-start = ((bf16[128,8,256]{0,2,1:T(8,128)(2,1)}), bf16[128,8,256]{0,2,1:T(8,128)(2,1)S(1)}, u32[]{:S(2)}, u32[]{:S(2)}) async-start(bf16[128,8,256]{0,2,1:T(8,128)(2,1)} %bitcast.3), calls=%async_computation | async-start | bytes 1048576 | tf_op jit(solution)/shard_map/all_to_all | solution.py:109
  22.1 13.7 %all-to-all-start.1 = ((bf16[128,8,256]{0,2,1:T(8,128)(2,1)}), bf16[128,8,256]{0,2,1:T(8,128)(2,1)S(1)}, u32[]{:S(2)}, u32[]{:S(2)}) async-start(bf16[128,8,256]{0,2,1:T(8,128)(2,1)} %bitcast.6), calls=%async_computation.1 | async-start | bytes 1048576 | tf_op jit(solution)/shard_map/all_to_all | solution.py:110
  35.8 13.7 %all-to-all-start.2 = ((bf16[128,8,256]{0,2,1:T(8,128)(2,1)}), bf16[128,8,256]{0,2,1:T(8,128)(2,1)S(1)}, u32[]{:S(2)}, u32[]{:S(2)}) async-start(bf16[128,8,256]{0,2,1:T(8,128)(2,1)} %bitcast.9), calls=%async_computation.2 | async-start | bytes 1048576 | tf_op jit(solution)/shard_map/all_to_all | solution.py:111
  43.2 10.1 %copy-start.7 = (bf16[8,128,256]{2,1,0:T(8,128)(2,1)}, bf16[8,128,256]{2,1,0:T(8,128)(2,1)S(1)}, u32[]{:S(2)}) copy-start(bf16[8,128,256]{2,1,0:T(8,128)(2,1)S(1)} %copy.75) | copy-start | bytes 1572868
  49.8 7.4 %copy-start.12 = (bf16[8,128,256]{2,1,0:T(8,128)(2,1)}, bf16[8,128,256]{2,1,0:T(8,128)(2,1)S(1)}, u32[]{:S(2)}) copy-start(bf16[8,128,256]{2,1,0:T(8,128)(2,1)S(1)} %copy.77) | copy-start | bytes 1572868
  50.5 5.1 %copy-start = (f32[1024,1024]{0,1:T(8,128)}, f32[1024,1024]{0,1:T(8,128)S(1)}, u32[]{:S(2)}) copy-start(f32[1024,1024]{0,1:T(8,128)S(1)} %fusion.21) | copy-start | bytes 12582916
  53.4 3.8 %copy-start.3 = (f32[1024,1024]{0,1:T(8,128)}, f32[1024,1024]{0,1:T(8,128)S(1)}, u32[]{:S(2)}) copy-start(f32[1024,1024]{0,1:T(8,128)S(1)} %get-tuple-element.23) | copy-start | bytes 12582916
  53.4 85.5 %copy-start.9 = (pred[1024,1024]{0,1:T(32,128)(4,1)}, pred[1024,1024]{0,1:T(32,128)(4,1)S(1)}, u32[]{:S(2)}) copy-start(pred[1024,1024]{0,1:T(32,128)(4,1)S(1)} %get-tuple-element.22) | copy-start | bytes 3145732
  59.6 13.7 %all-to-all-start.3 = ((bf16[8,128,256]{1,2,0:T(8,128)(2,1)}), bf16[8,128,256]{1,2,0:T(8,128)(2,1)S(1)}, u32[]{:S(2)}, u32[]{:S(2)}) async-start(bf16[8,128,256]{1,2,0:T(8,128)(2,1)} %copy_bitcast_fusion.3), calls=%async_computation.3 | async-start | bytes 1048576 | tf_op jit(solution)/shard_map/all_to_all | solution.py:128
  66.2 19.7 %copy-start.18 = (s32[1,4]{1,0:T(1,128)S(1)}, s32[1,4]{1,0:T(1,128)}, u32[]{:S(2)}) copy-start(s32[1,4]{1,0:T(1,128)} %param.15) | copy-start | bytes 52
  87.8 20.3 %all-to-all-start.5 = ((f32[32,1,1]{2,1,0:T(1,128)}), f32[32,1,1]{2,1,0:T(1,128)S(1)}, u32[]{:S(2)}, u32[]{:S(2)}) async-start(f32[32,1,1]{2,1,0:T(1,128)} %broadcast_in_dim.23), calls=%async_computation.5 | async-start | bytes 32768 | tf_op jit(solution)/shard_map/all_to_all | solution.py:19
  98.4 35.5 %all-gather.2.cloned.1.call-start = ((), (), s32[]{:S(2)}) async-start(), calls=%async_computation.11 | async-start | bytes 3538944 | tf_op jit(solution)/shard_map/all_gather | solution.py:149
  110.5 73.3 %reduce-scatter.3.cloned.1.call-start = ((), (), s32[]{:S(2)}) async-start(), calls=%async_computation.12 | async-start | bytes 884736 | tf_op jit(solution)/shard_map/reduce_scatter | solution.py:30
  133.9 3.4 %copy-start.4 = (f32[1024,1024]{0,1:T(8,128)S(1)}, f32[1024,1024]{0,1:T(8,128)}, u32[]{:S(2)}) copy-start(f32[1024,1024]{0,1:T(8,128)} %copy-done.3) | copy-start | bytes 12582916
  137.3 3.9 %copy-start.14 = (bf16[1024,256]{0,1:T(8,128)(2,1)}, bf16[1024,256]{0,1:T(8,128)(2,1)S(1)}, u32[]{:S(2)}) copy-start(bf16[1024,256]{0,1:T(8,128)(2,1)S(1)} %convolution_convert_fusion) | copy-start | bytes 1572868
  137.3 2.4 %copy-start.1 = (f32[1024,1024]{0,1:T(8,128)S(1)}, f32[1024,1024]{0,1:T(8,128)}, u32[]{:S(2)}) copy-start(f32[1024,1024]{0,1:T(8,128)} %copy-done) | copy-start | bytes 12582916
  139.7 1.9 copy-start.19
  144.8 14.8 %all-to-all-start.8 = ((bf16[8,128,256]{1,2,0:T(8,128)(2,1)}), bf16[8,128,256]{1,2,0:T(8,128)(2,1)S(1)}, u32[]{:S(2)}, u32[]{:S(2)}) async-start(bf16[8,128,256]{1,2,0:T(8,128)(2,1)} %copy_bitcast_fusion), calls=%async_computation.8 | async-start | bytes 1048576 | tf_op jit(solution)/shard_map/all_to_all | solution.py:182
  150.2 5.1 %copy-start.2 = (f32[1024,1024]{0,1:T(8,128)S(1)}, f32[1024,1024]{0,1:T(8,128)}, u32[]{:S(2)}) copy-start(f32[1024,1024]{0,1:T(8,128)} %copy-done) | copy-start | bytes 12582916
  150.2 5.1 %copy-start.10 = (pred[1024,1024]{0,1:T(32,128)(4,1)S(1)}, pred[1024,1024]{0,1:T(32,128)(4,1)}, u32[]{:S(2)}) copy-start(pred[1024,1024]{0,1:T(32,128)(4,1)} %copy-done.9) | copy-start | bytes 3145732
  150.2 5.2 %copy-start.13 = (bf16[8,128,256]{2,1,0:T(8,128)(2,1)S(1)}, bf16[8,128,256]{2,1,0:T(8,128)(2,1)}, u32[]{:S(2)}) copy-start(bf16[8,128,256]{2,1,0:T(8,128)(2,1)} %copy-done.12) | copy-start | bytes 1572868
  150.2 5.2 %copy-start.15 = (bf16[1024,256]{0,1:T(8,128)(2,1)S(1)}, bf16[1024,256]{0,1:T(8,128)(2,1)}, u32[]{:S(2)}) copy-start(bf16[1024,256]{0,1:T(8,128)(2,1)} %copy-done.14) | copy-start | bytes 1572868
  157.1 1.7 copy-start.5
  159.7 12.0 %all-to-all-start.7 = ((bf16[8,128,256]{1,2,0:T(8,128)(2,1)}), bf16[8,128,256]{1,2,0:T(8,128)(2,1)S(1)}, u32[]{:S(2)}, u32[]{:S(2)}) async-start(bf16[8,128,256]{1,2,0:T(8,128)(2,1)} %copy_bitcast_fusion.1), calls=%async_computation.7 | async-start | bytes 1048576 | tf_op jit(solution)/shard_map/all_to_all | solution.py:179
  164.5 1.7 copy-start.6
  164.5 1.8 copy-start.8
  171.6 14.2 %all-to-all-start.6 = ((bf16[8,128,256]{1,2,0:T(8,128)(2,1)}), bf16[8,128,256]{1,2,0:T(8,128)(2,1)S(1)}, u32[]{:S(2)}, u32[]{:S(2)}) async-start(bf16[8,128,256]{1,2,0:T(8,128)(2,1)} %copy_bitcast_fusion.2), calls=%async_computation.6 | async-start | bytes 1048576 | tf_op jit(solution)/shard_map/all_to_all | solution.py:176
  178.2 29.9 %reduce-scatter.5.cloned.1.call-start = ((), (), s32[]{:S(2)}) async-start(), calls=%async_computation.13 | async-start | bytes 122880 | tf_op jit(solution)/shard_map/reduce_scatter | solution.py:30
Sparse Core Ops, SparseCore 0:
  110.6 23.2 all-gather.1
  144.0 39.6 reduce-scatter.2
  186.3 21.8 reduce-scatter.4
where the time goes:
time: 217 us; the launch traced here: 216 us
  waiting for transfers between devices  87.8 us (40%)
  starting transfers between devices  53 us (24%)
  matrix products  29.4 us (14%)
  between operations  15.4 us (7%)
  local copies, waits for them, and re-layouts  11.8 us (5%)
  other arithmetic  10.1 us (5%)
  blocking collectives  8.45 us (4%)
    reduce_scatter x2, waiting for transfers between devices, summed_rows(): nearer = lax.psum_scatter(array, axes[0], scatter_dimension=dim, tiled=True)  26.9 us
    all_gather x1, waiting for transfers between devices, on_device(): pred_pack = lax.all_gather(pred_grad, 'ctx', axis=0, tiled=True)  23.2 us
    all_to_all x1, starting transfers between devices, sent_to_all(): return lax.all_to_all(copies, axis, split_axis=0, concat_axis=0, tiled=True)  10.7 us
    unnamed x46, local copies, waits for them, and re-layouts  9.48 us
    all_to_all x1, waiting for transfers between devices, sent_to_all(): return lax.all_to_all(copies, axis, split_axis=0, concat_axis=0, tiled=True)  8.99 us
    all_to_all x1, blocking collectives, sent_to_all(): return lax.all_to_all(copies, axis, split_axis=0, concat_axis=0, tiled=True)  8.45 us
    all_to_all x1, waiting for transfers between devices, on_device(): lax.all_to_all(out_head, 'ctx', split_axis=0, concat_axis=1, tiled=True)  7.07 us
    dot_general x2, matrix products, head_backward(): lax.dot_general(grad_head, value_head, (((1,), (1,)), ((), ())), preferre...  6.82 us
  transfers between devices with their start and end apart: 11, of which 9 were waited for; matrix products, arithmetic and copies ran while one was open for 9% of the time, Pallas kernels for 0%

commit v1 on v0

--- a/solution.py
+++ b/solution.py
@@ -146,7 +146,9 @@
     row_scale = jnp.sum(onehot * clip_scale[None, :], axis=1)
     pred_grad = (residue * row_scale[:, None]).astype(jnp.bfloat16)
     norm_factor = 1.0 / math.sqrt(tokens_all)
-    pred_pack = lax.all_gather(pred_grad, "ctx", axis=0, tiled=True)
+    pred_pack = jnp.concatenate(
+        lax.all_to_all(jnp.stack([pred_grad] * lax.axis_size("ctx")), "ctx", 0, 0), axis=0
+    )
     w_block = lax.dynamic_slice_in_dim(w_out, ctx_place * width_dev, width_dev, 0)
     grad_head = lax.dot_general(
         pred_pack, w_block, (((1,), (1,)), ((), ())), preferred_element_type=jnp.float32

time: 217 us -> 239 us (1.10)
  starting transfers between devices: 53 us -> 62.7 us
  waiting for transfers between devices: 87.8 us -> 93.9 us
  matrix products: 29.4 us -> 34.8 us
    all_to_all x0 -> x1, waiting for transfers between devices: none -> 35.4 us  [on_device(): lax.all_to_all(jnp.stack([pred_grad] * lax.axis_size('ctx')), 'ctx', 0, 0)]
    all_gather x1 -> x0, waiting for transfers between devices: 23.2 us -> none  [on_device(): pred_pack = lax.all_gather(pred_grad, 'ctx', axis=0, tiled=True)]
    reduce_scatter x2, waiting for transfers between devices: 26.9 us -> 12.8 us  [summed_rows(): nearer = lax.psum_scatter(array, axes[0], scatter_dimension=dim, tiled=True)]
    all_to_all x0 -> x1, starting transfers between devices: none -> 6.75 us  [on_device(): lax.all_to_all(jnp.stack([pred_grad] * lax.axis_size('ctx')), 'ctx', 0, 0)]
    all_to_all x1, waiting for transfers between devices: 0.01 us -> 4.41 us  [on_device(): lax.all_to_all(jnp.concatenate(parts_q, axis=1), 'ctx', split_axis=0, con...]
    all_to_all x1, waiting for transfers between devices: 0.01 us -> 3.02 us  [on_device(): lax.all_to_all(jnp.concatenate(parts_v, axis=1), 'ctx', split_axis=0, con...]
    unnamed x46 -> x44, local copies, waits for them, and re-layouts: 9.48 us -> 8.99 us
  transfers between devices with their start and end apart: 11 -> 11, of which waited for: 9 -> 10; matrix products, arithmetic and copies ran while one was open for 9% -> 10% of each run, Pallas kernels for 0% -> 0%
where the time goes in v1:
time: 239 us; the launch traced here: 238 us
  waiting for transfers between devices  93.9 us (39%)
  starting transfers between devices  62.7 us (26%)
  matrix products  34.8 us (15%)
  between operations  15.7 us (7%)
  local copies, waits for them, and re-layouts  13.3 us (6%)
  other arithmetic  9.37 us (4%)
  blocking collectives  8.45 us (4%)
    all_to_all x1, waiting for transfers between devices, on_device(): lax.all_to_all(jnp.stack([pred_grad] * lax.axis_size('ctx')), 'ctx', 0, 0)  35.4 us
    reduce_scatter x2, waiting for transfers between devices, summed_rows(): nearer = lax.psum_scatter(array, axes[0], scatter_dimension=dim, tiled=True)  12.8 us
    all_to_all x1, starting transfers between devices, sent_to_all(): return lax.all_to_all(copies, axis, split_axis=0, concat_axis=0, tiled=True)  10.8 us
    unnamed x44, local copies, waits for them, and re-layouts  8.99 us
    all_to_all x1, waiting for transfers between devices, sent_to_all(): return lax.all_to_all(copies, axis, split_axis=0, concat_axis=0, tiled=True)  8.86 us
    all_to_all x1, blocking collectives, sent_to_all(): return lax.all_to_all(copies, axis, split_axis=0, concat_axis=0, tiled=True)  8.45 us
    dot_general x2, matrix products, head_backward(): lax.dot_general(grad_head, value_head, (((1,), (1,)), ((), ())), preferre...  8.12 us
    all_to_all x1, waiting for transfers between devices, on_device(): lax.all_to_all(out_head, 'ctx', split_axis=0, concat_axis=1, tiled=True)  7.07 us
  transfers between devices with their start and end apart: 11, of which 10 were waited for; matrix products, arithmetic and copies ran while one was open for 10% of the time, Pallas kernels for 0%

profile of v1, /device:TPU:4, one launch (start us, length us, event | category | flops | bytes accessed | tf_op | source)
XLA Modules:
  0.0 238.3 jit_solution(6322683524384532719)
XLA Ops:
  7.2 2.1 copy.72
  9.3 5.6 %all-to-all-start = ((bf16[128,8,256]{0,2,1:T(8,128)(2,1)}), bf16[128,8,256]{0,2,1:T(8,128)(2,1)S(1)}, u32[]{:S(2)}, u32[]{:S(2)}) async-start(bf16[128,8,256]{0,2,1:T(8,128)(2,1)} %bitcast.3), calls=%async_computation | async-start | bytes 1048576 | tf_op jit(solution)/shard_map/all_to_all | solution.py:109
  14.9 2.0 copy.74
  17.0 5.1 %all-to-all-done = bf16[128,8,256]{0,2,1:T(8,128)(2,1)S(1)} async-done(((bf16[128,8,256]{0,2,1:T(8,128)(2,1)}), bf16[128,8,256]{0,2,1:T(8,128)(2,1)S(1)}, u32[]{:S(2)}, u32[]{:S(2)}) %all-to-all-start) | async-done | bytes 524320 | tf_op jit(solution)/shard_map/all_to_all | solution.py:109
  22.1 6.6 %all-to-all-start.1 = ((bf16[128,8,256]{0,2,1:T(8,128)(2,1)}), bf16[128,8,256]{0,2,1:T(8,128)(2,1)S(1)}, u32[]{:S(2)}, u32[]{:S(2)}) async-start(bf16[128,8,256]{0,2,1:T(8,128)(2,1)} %bitcast.6), calls=%async_computation.1 | async-start | bytes 1048576 | tf_op jit(solution)/shard_map/all_to_all | solution.py:110
  29.7 6.2 %all-to-all-done.1 = bf16[128,8,256]{0,2,1:T(8,128)(2,1)S(1)} async-done(((bf16[128,8,256]{0,2,1:T(8,128)(2,1)}), bf16[128,8,256]{0,2,1:T(8,128)(2,1)S(1)}, u32[]{:S(2)}, u32[]{:S(2)}) %all-to-all-start.1) | async-done | bytes 524320 | tf_op jit(solution)/shard_map/all_to_all | solution.py:110
  35.8 6.6 %all-to-all-start.2 = ((bf16[128,8,256]{0,2,1:T(8,128)(2,1)}), bf16[128,8,256]{0,2,1:T(8,128)(2,1)S(1)}, u32[]{:S(2)}, u32[]{:S(2)}) async-start(bf16[128,8,256]{0,2,1:T(8,128)(2,1)} %bitcast.9), calls=%async_computation.2 | async-start | bytes 1048576 | tf_op jit(solution)/shard_map/all_to_all | solution.py:111
  43.2 6.3 %all-to-all-done.2 = bf16[128,8,256]{0,2,1:T(8,128)(2,1)S(1)} async-done(((bf16[128,8,256]{0,2,1:T(8,128)(2,1)}), bf16[128,8,256]{0,2,1:T(8,128)(2,1)S(1)}, u32[]{:S(2)}, u32[]{:S(2)}) %all-to-all-start.2) | async-done | bytes 524320 | tf_op jit(solution)/shard_map/all_to_all | solution.py:111
  50.9 2.5 %fusion.1 = (f32[1024]{0:T(1024)S(1)}, f32[1024]{0:T(1024)S(1)}, pred[1024,1024]{0,1:T(32,128)(4,1)S(1)}, f32[1024,1024]{0,1:T(8,128)S(1)}) fusion(f32[1024,1024]{0,1:T(8,128)S(1)} %fusion.21, s32[1024]{0:T(1024)S(1)} %add_select_fusion, pred[128,8,8,128]{3,2,1,0:T(8,128)(4,1)S(1)} %bitcast.97, s32[1024]{0:T(1024)S(1)} %convert_reduce_fusion, ...), kind=kOutput, calls=%fused_computation.8 | convolution fusion | flops 278919168 | bytes 11034624 | tf_op jit(solution)/shard_map/dot_general | solution.py:55
  53.4 2.2 fusion.5
  59.6 6.6 %all-to-all-start.3 = ((bf16[8,128,256]{1,2,0:T(8,128)(2,1)}), bf16[8,128,256]{1,2,0:T(8,128)(2,1)S(1)}, u32[]{:S(2)}, u32[]{:S(2)}) async-start(bf16[8,128,256]{1,2,0:T(8,128)(2,1)} %copy_bitcast_fusion.3), calls=%async_computation.3 | async-start | bytes 1048576 | tf_op jit(solution)/shard_map/all_to_all | solution.py:128
  66.3 7.1 %all-to-all-done.3 = bf16[8,128,256]{1,2,0:T(8,128)(2,1)S(1)} async-done(((bf16[8,128,256]{1,2,0:T(8,128)(2,1)}), bf16[8,128,256]{1,2,0:T(8,128)(2,1)S(1)}, u32[]{:S(2)}, u32[]{:S(2)}) %all-to-all-start.3) | async-done | bytes 524320 | tf_op jit(solution)/shard_map/all_to_all | solution.py:128
  73.4 3.9 %multiply_reduce_fusion = (f32[128]{0:T(128)S(1)}, f32[128,1536]{1,0:T(8,128)S(1)}) fusion(bf16[128,1536]{1,0:T(8,128)(2,1)} %param.12, bf16[128,2048]{0,1:T(8,128)(2,1)S(1)} %bitcast.86, bf16[2048,1536]{1,0:T(8,128)(2,1)} %param.13), kind=kOutput, calls=%fused_computation.36 | convolution fusion | flops 806092672 | bytes 7995904 | tf_op jit(solution)/shard_map/dot_general | solution.py:129
  77.4 8.4 %all_to_all.150 = f32[8,1,4]{2,1,0:T(1,128)S(1)} all-to-all(f32[8,1,4]{2,1,0:T(1,128)S(1)} %broadcast_in_dim.22), channel_id=1, replica_groups=mesh['dp_0'=8,'dp_1'=4,'ctx'=8] {'ctx'}, dimensions={0} | all-to-all | bytes 256 | tf_op jit(solution)/shard_map/all_to_all | solution.py:19
  87.8 10.8 %all-to-all-start.5 = ((f32[32,1,1]{2,1,0:T(1,128)}), f32[32,1,1]{2,1,0:T(1,128)S(1)}, u32[]{:S(2)}, u32[]{:S(2)}) async-start(f32[32,1,1]{2,1,0:T(1,128)} %broadcast_in_dim.23), calls=%async_computation.5 | async-start | bytes 32768 | tf_op jit(solution)/shard_map/all_to_all | solution.py:19
  99.3 8.9 %all-to-all-done.5 = f32[32,1,1]{2,1,0:T(1,128)S(1)} async-done(((f32[32,1,1]{2,1,0:T(1,128)}), f32[32,1,1]{2,1,0:T(1,128)S(1)}, u32[]{:S(2)}, u32[]{:S(2)}) %all-to-all-start.5) | async-done | bytes 160 | tf_op jit(solution)/shard_map/all_to_all | solution.py:19
  109.7 2.0 stack.2
  111.8 6.8 %all-to-all-start.6 = ((bf16[8,128,1536]{2,1,0:T(8,128)(2,1)}), bf16[8,128,1536]{2,1,0:T(8,128)(2,1)}, u32[]{:S(2)}, u32[]{:S(2)}) async-start(bf16[8,128,1536]{2,1,0:T(8,128)(2,1)} %stack.2), calls=%async_computation.6 | async-start | bytes 6291456 | tf_op jit(solution)/shard_map/all_to_all | solution.py:150
  118.5 35.4 %all-to-all-done.6 = bf16[8,128,1536]{2,1,0:T(8,128)(2,1)} async-done(((bf16[8,128,1536]{2,1,0:T(8,128)(2,1)}), bf16[8,128,1536]{2,1,0:T(8,128)(2,1)}, u32[]{:S(2)}, u32[]{:S(2)}) %all-to-all-start.6) | async-done | bytes 3145760 | tf_op jit(solution)/shard_map/all_to_all | solution.py:150
  153.9 4.1 %fusion.3 = bf16[256,1536]{0,1:T(8,128)(2,1)} fusion(bf16[1024,1536]{1,0:T(8,128)(2,1)} %bitcast.19, bf16[1024,128]{0,1:T(8,128)(2,1)S(1)} %convolution_convert_fusion.3, bf16[1024,128]{0,1:T(8,128)(2,1)S(1)} %convolution_convert_fusion.4), kind=kOutput, calls=%fused_computation.11 | convolution fusion | flops 807141376 | bytes 4456448 | tf_op jit(solution)/shard_map/dot_general | solution.py:157
  158.0 3.2 %convolution_convert_fusion = bf16[1024,256]{0,1:T(8,128)(2,1)S(1)} fusion(bf16[1024,1536]{1,0:T(8,128)(2,1)} %bitcast.19, bf16[2048,1536]{1,0:T(8,128)(2,1)} %param.13, s32[]{:T(128)S(6)} %select_n.38), kind=kOutput, calls=%fused_computation.17 | convolution fusion | flops 805568512 | bytes 4456452 | tf_op jit(solution)/shard_map/dot_general | solution.py:153
  163.6 2.3 convolution_convert_fusion.1
  166.0 5.0 %multiply_convert_fusion.1 = bf16[1024,1024]{0,1:T(8,128)(2,1)S(1)} fusion(f32[1024]{0:T(1024)S(1)} %get-tuple-element.20, bf16[1024,256]{1,0:T(8,128)(2,1)S(1)} %bitcast.100, bf16[1024,256]{0,1:T(8,128)(2,1)} %copy-done.13, f32[1024]{0:T(1024)S(1)} %get-tuple-element.16, pred[1024,1024]{0,1:T(32,128)(4,1)} %copy-done.8, f32[1024]{0:T(1024)S(1)} %get-tuple-element.18, ...), kind=kOutput, calls=%fused_computation.1 | convolution fusion | flops 276824064 | bytes 7876608 | tf_op jit(solution)/shard_map/dot_general | solution.py:74
  171.0 3.1 %multiply_convert_fusion = bf16[1024,1024]{0,1:T(8,128)(2,1)} fusion(f32[1024]{0:T(1024)S(1)} %get-tuple-element.21, bf16[1024,256]{1,0:T(8,128)(2,1)S(1)} %bitcast.101, bf16[1024,256]{0,1:T(8,128)(2,1)S(1)} %copy-done.14, f32[1024]{0:T(1024)S(1)} %get-tuple-element.17, pred[1024,1024]{0,1:T(32,128)(4,1)S(1)} %copy-done.9, f32[1024]{0:T(1024)S(1)} %get-tuple-element.19, ...), kind=kOutput, calls=%fused_computation | convolution fusion | flops 276824064 | bytes 7876608 | tf_op jit(solution)/shard_map/dot_general | solution.py:74
  175.0 6.6 %all-to-all-start.9 = ((bf16[8,128,256]{1,2,0:T(8,128)(2,1)}), bf16[8,128,256]{1,2,0:T(8,128)(2,1)S(1)}, u32[]{:S(2)}, u32[]{:S(2)}) async-start(bf16[8,128,256]{1,2,0:T(8,128)(2,1)} %copy_bitcast_fusion), calls=%async_computation.9 | async-start | bytes 1048576 | tf_op jit(solution)/shard_map/all_to_all | solution.py:184
  182.4 2.4 %fusion.11 = bf16[1024,128]{0,1:T(8,128)(2,1)S(1)} fusion(bf16[1024,1024]{0,1:T(8,128)(2,1)} %multiply_convert_fusion, bf16[1024,256]{1,0:T(8,128)(2,1)S(1)} %bitcast.85), kind=kOutput, calls=%fused_computation.29 | convolution fusion | flops 268697600 | bytes 2621440 | tf_op jit(solution)/shard_map/dot_general | solution.py:83
  185.7 3.0 %all-to-all-done.9 = bf16[8,128,256]{1,2,0:T(8,128)(2,1)S(1)} async-done(((bf16[8,128,256]{1,2,0:T(8,128)(2,1)}), bf16[8,128,256]{1,2,0:T(8,128)(2,1)S(1)}, u32[]{:S(2)}, u32[]{:S(2)}) %all-to-all-start.9) | async-done | bytes 524320 | tf_op jit(solution)/shard_map/all_to_all | solution.py:184
  188.7 6.6 %all-to-all-start.8 = ((bf16[8,128,256]{1,2,0:T(8,128)(2,1)}), bf16[8,128,256]{1,2,0:T(8,128)(2,1)S(1)}, u32[]{:S(2)}, u32[]{:S(2)}) async-start(bf16[8,128,256]{1,2,0:T(8,128)(2,1)} %copy_bitcast_fusion.1), calls=%async_computation.8 | async-start | bytes 1048576 | tf_op jit(solution)/shard_map/all_to_all | solution.py:181
  198.5 4.0 %all-to-all-done.8 = bf16[8,128,256]{1,2,0:T(8,128)(2,1)S(1)} async-done(((bf16[8,128,256]{1,2,0:T(8,128)(2,1)}), bf16[8,128,256]{1,2,0:T(8,128)(2,1)S(1)}, u32[]{:S(2)}, u32[]{:S(2)}) %all-to-all-start.8) | async-done | bytes 524320 | tf_op jit(solution)/shard_map/all_to_all | solution.py:181
  202.5 6.6 %all-to-all-start.7 = ((bf16[8,128,256]{1,2,0:T(8,128)(2,1)}), bf16[8,128,256]{1,2,0:T(8,128)(2,1)S(1)}, u32[]{:S(2)}, u32[]{:S(2)}) async-start(bf16[8,128,256]{1,2,0:T(8,128)(2,1)} %copy_bitcast_fusion.2), calls=%async_computation.7 | async-start | bytes 1048576 | tf_op jit(solution)/shard_map/all_to_all | solution.py:178
  211.8 4.4 %all-to-all-done.7 = bf16[8,128,256]{1,2,0:T(8,128)(2,1)S(1)} async-done(((bf16[8,128,256]{1,2,0:T(8,128)(2,1)}), bf16[8,128,256]{1,2,0:T(8,128)(2,1)S(1)}, u32[]{:S(2)}, u32[]{:S(2)}) %all-to-all-start.7) | async-done | bytes 524320 | tf_op jit(solution)/shard_map/all_to_all | solution.py:178
  217.2 12.8 %reduce-scatter.5.cloned.1.call-done = bf16[256,48]{0,1:T(8,128)(2,1)} async-done(((bf16[256,192]{0,1:T(8,128)(2,1)}), bf16[256,48]{0,1:T(8,128)(2,1)}) %reduce-scatter.5.cloned.1.call-update) | async-done | bytes 24592 | tf_op jit(solution)/shard_map/reduce_scatter | solution.py:30
  (80 shorter events, 23.3 us)
Async XLA Ops:
  7.2 21.5 %copy-start.10 = (bf16[128,2048]{1,0:T(8,128)(2,1)S(1)}, bf16[128,2048]{1,0:T(8,128)(2,1)}, u32[]{:S(2)}) copy-start(bf16[128,2048]{1,0:T(8,128)(2,1)} %param.11) | copy-start | bytes 1572868
  7.2 35.2 %copy-start.16 = (s32[1,8,8]{2,1,0:T(8,128)S(1)}, s32[1,8,8]{2,1,0:T(8,128)}, u32[]{:S(2)}) copy-start(s32[1,8,8]{2,1,0:T(8,128)} %param.16) | copy-start | bytes 772
  7.2 35.3 %copy-start.17 = (s32[1,4]{1,0:T(1,128)S(1)}, s32[1,4]{1,0:T(1,128)}, u32[]{:S(2)}) copy-start(s32[1,4]{1,0:T(1,128)} %param.14) | copy-start | bytes 52
  9.3 12.8 %all-to-all-start = ((bf16[128,8,256]{0,2,1:T(8,128)(2,1)}), bf16[128,8,256]{0,2,1:T(8,128)(2,1)S(1)}, u32[]{:S(2)}, u32[]{:S(2)}) async-start(bf16[128,8,256]{0,2,1:T(8,128)(2,1)} %bitcast.3), calls=%async_computation | async-start | bytes 1048576 | tf_op jit(solution)/shard_map/all_to_all | solution.py:109
  22.1 13.7 %all-to-all-start.1 = ((bf16[128,8,256]{0,2,1:T(8,128)(2,1)}), bf16[128,8,256]{0,2,1:T(8,128)(2,1)S(1)}, u32[]{:S(2)}, u32[]{:S(2)}) async-start(bf16[128,8,256]{0,2,1:T(8,128)(2,1)} %bitcast.6), calls=%async_computation.1 | async-start | bytes 1048576 | tf_op jit(solution)/shard_map/all_to_all | solution.py:110
  35.8 13.7 %all-to-all-start.2 = ((bf16[128,8,256]{0,2,1:T(8,128)(2,1)}), bf16[128,8,256]{0,2,1:T(8,128)(2,1)S(1)}, u32[]{:S(2)}, u32[]{:S(2)}) async-start(bf16[128,8,256]{0,2,1:T(8,128)(2,1)} %bitcast.9), calls=%async_computation.2 | async-start | bytes 1048576 | tf_op jit(solution)/shard_map/all_to_all | solution.py:111
  43.2 10.1 %copy-start.6 = (bf16[8,128,256]{2,1,0:T(8,128)(2,1)}, bf16[8,128,256]{2,1,0:T(8,128)(2,1)S(1)}, u32[]{:S(2)}) copy-start(bf16[8,128,256]{2,1,0:T(8,128)(2,1)S(1)} %copy.75) | copy-start | bytes 1572868
  49.8 7.4 %copy-start.11 = (bf16[8,128,256]{2,1,0:T(8,128)(2,1)}, bf16[8,128,256]{2,1,0:T(8,128)(2,1)S(1)}, u32[]{:S(2)}) copy-start(bf16[8,128,256]{2,1,0:T(8,128)(2,1)S(1)} %copy.77) | copy-start | bytes 1572868
  50.5 6.7 %copy-start = (f32[1024,1024]{0,1:T(8,128)}, f32[1024,1024]{0,1:T(8,128)S(1)}, u32[]{:S(2)}) copy-start(f32[1024,1024]{0,1:T(8,128)S(1)} %fusion.21) | copy-start | bytes 12582916
  53.4 2.3 copy-start.3
  53.4 109.6 %copy-start.8 = (pred[1024,1024]{0,1:T(32,128)(4,1)}, pred[1024,1024]{0,1:T(32,128)(4,1)S(1)}, u32[]{:S(2)}) copy-start(pred[1024,1024]{0,1:T(32,128)(4,1)S(1)} %get-tuple-element.22) | copy-start | bytes 3145732
  59.6 13.7 %all-to-all-start.3 = ((bf16[8,128,256]{1,2,0:T(8,128)(2,1)}), bf16[8,128,256]{1,2,0:T(8,128)(2,1)S(1)}, u32[]{:S(2)}, u32[]{:S(2)}) async-start(bf16[8,128,256]{1,2,0:T(8,128)(2,1)} %copy_bitcast_fusion.3), calls=%async_computation.3 | async-start | bytes 1048576 | tf_op jit(solution)/shard_map/all_to_all | solution.py:128
  66.2 19.7 %copy-start.18 = (s32[1,4]{1,0:T(1,128)S(1)}, s32[1,4]{1,0:T(1,128)}, u32[]{:S(2)}) copy-start(s32[1,4]{1,0:T(1,128)} %param.15) | copy-start | bytes 52
  87.8 20.4 %all-to-all-start.5 = ((f32[32,1,1]{2,1,0:T(1,128)}), f32[32,1,1]{2,1,0:T(1,128)S(1)}, u32[]{:S(2)}, u32[]{:S(2)}) async-start(f32[32,1,1]{2,1,0:T(1,128)} %broadcast_in_dim.23), calls=%async_computation.5 | async-start | bytes 32768 | tf_op jit(solution)/shard_map/all_to_all | solution.py:19
  111.8 42.1 %all-to-all-start.6 = ((bf16[8,128,1536]{2,1,0:T(8,128)(2,1)}), bf16[8,128,1536]{2,1,0:T(8,128)(2,1)}, u32[]{:S(2)}, u32[]{:S(2)}) async-start(bf16[8,128,1536]{2,1,0:T(8,128)(2,1)} %stack.2), calls=%async_computation.6 | async-start | bytes 6291456 | tf_op jit(solution)/shard_map/all_to_all | solution.py:150
  118.5 90.6 %reduce-scatter.3.cloned.1.call-start = ((), (), s32[]{:S(2)}) async-start(), calls=%async_computation.12 | async-start | bytes 884736 | tf_op jit(solution)/shard_map/reduce_scatter | solution.py:30
  158.0 3.4 %copy-start.4 = (f32[1024,1024]{0,1:T(8,128)S(1)}, f32[1024,1024]{0,1:T(8,128)}, u32[]{:S(2)}) copy-start(f32[1024,1024]{0,1:T(8,128)} %copy-done.3) | copy-start | bytes 12582916
  161.2 1.8 copy-start.13
  161.4 2.2 copy-start.1
  163.6 2.3 copy-start.12
  165.9 5.1 %copy-start.2 = (f32[1024,1024]{0,1:T(8,128)S(1)}, f32[1024,1024]{0,1:T(8,128)}, u32[]{:S(2)}) copy-start(f32[1024,1024]{0,1:T(8,128)} %copy-done) | copy-start | bytes 12582916
  165.9 5.1 %copy-start.9 = (pred[1024,1024]{0,1:T(32,128)(4,1)S(1)}, pred[1024,1024]{0,1:T(32,128)(4,1)}, u32[]{:S(2)}) copy-start(pred[1024,1024]{0,1:T(32,128)(4,1)} %copy-done.8) | copy-start | bytes 3145732
  165.9 5.1 %copy-start.14 = (bf16[1024,256]{0,1:T(8,128)(2,1)S(1)}, bf16[1024,256]{0,1:T(8,128)(2,1)}, u32[]{:S(2)}) copy-start(bf16[1024,256]{0,1:T(8,128)(2,1)} %copy-done.13) | copy-start | bytes 1572868
  171.0 3.1 %copy-start.15 = (bf16[1024,128]{0,1:T(8,128)(2,1)S(1)}, bf16[1024,128]{0,1:T(8,128)(2,1)}, u32[]{:S(2)}) copy-start(bf16[1024,128]{0,1:T(8,128)(2,1)} %convolution_convert_fusion.1) | copy-start | bytes 786436
  175.0 13.7 %all-to-all-start.9 = ((bf16[8,128,256]{1,2,0:T(8,128)(2,1)}), bf16[8,128,256]{1,2,0:T(8,128)(2,1)S(1)}, u32[]{:S(2)}, u32[]{:S(2)}) async-start(bf16[8,128,256]{1,2,0:T(8,128)(2,1)} %copy_bitcast_fusion), calls=%async_computation.9 | async-start | bytes 1048576 | tf_op jit(solution)/shard_map/all_to_all | solution.py:184
  188.7 13.7 %all-to-all-start.8 = ((bf16[8,128,256]{1,2,0:T(8,128)(2,1)}), bf16[8,128,256]{1,2,0:T(8,128)(2,1)S(1)}, u32[]{:S(2)}, u32[]{:S(2)}) async-start(bf16[8,128,256]{1,2,0:T(8,128)(2,1)} %copy_bitcast_fusion.1), calls=%async_computation.8 | async-start | bytes 1048576 | tf_op jit(solution)/shard_map/all_to_all | solution.py:181
  195.3 1.7 copy-start.5
  195.3 1.8 copy-start.7
  202.5 13.7 %all-to-all-start.7 = ((bf16[8,128,256]{1,2,0:T(8,128)(2,1)}), bf16[8,128,256]{1,2,0:T(8,128)(2,1)S(1)}, u32[]{:S(2)}, u32[]{:S(2)}) async-start(bf16[8,128,256]{1,2,0:T(8,128)(2,1)} %copy_bitcast_fusion.2), calls=%async_computation.7 | async-start | bytes 1048576 | tf_op jit(solution)/shard_map/all_to_all | solution.py:178
  209.1 21.0 %reduce-scatter.5.cloned.1.call-start = ((), (), s32[]{:S(2)}) async-start(), calls=%async_computation.13 | async-start | bytes 122880 | tf_op jit(solution)/shard_map/reduce_scatter | solution.py:30
Sparse Core Ops, SparseCore 0:
  166.0 33.5 reduce-scatter.2
  212.4 17.6 reduce-scatter.4
